TPU v7x, 128 devices: a whole 4x4x4 slice. The times are simulated.
128 devices in a mesh: bead: 32 (over x, y, z_lo), space: 4 (over z_hi, core).
Axes of the slice: x: 4, y: 4, z: 4 (z_hi: 2, z_lo: 2; z = z_hi * 2 + z_lo), core: 2. Of those that a mesh axis runs over, the one named last changes fastest.
Arguments:
- positions: float32 [32, 3, 32768], P('bead', None, 'space'), may hold values from -6 to 6
- momenta: float32 [32, 3, 32768], P('bead', None, 'space'), may hold values from -6 to 6
- forces: float32 [32, 3, 32768], P('bead', None, 'space'), may hold values from -6 to 6
- gle_drift: float32 [32, 5, 5], replicated, may hold values from -0.25 to 0.98, as said below
- gle_noise_mix: float32 [32, 5, 5], replicated, may hold values from -1.5 to 1.5
- aux_momenta: float32 [32, 4, 3, 32768], P(None, None, None, ('space', 'bead')), may hold values from -6 to 6
- noise: float32 [2, 32, 5, 3, 32768], P(None, None, None, None, ('space', 'bead')), may hold values from -6 to 6
Outputs:
- positions_out: float32 [32, 3, 32768], P('bead', None, 'space')
- momenta_out: float32 [32, 3, 32768], P('bead', None, 'space')
- forces_out: float32 [32, 3, 32768], P('bead', None, 'space')
- aux_out: float32 [32, 4, 3, 32768], P(None, None, None, ('space', 'bead'))
Inputs may be any that keep to these rules, and one draw needn't show every extreme that they name: `gle_drift`: one matrix a mode; diagonal entries positive.
All inputs are finite; a program needn't handle non-finite values.
Results may differ from a plain program's by a relative error of at most 0.00012.
Values sent between devices are 32-bit elements; how exact they have to be, the bound alone decides.
A program may use at most 64 MiB of HBM per device.

v0:
```python
import math

import jax
import jax.numpy as jnp
import numpy as np
from jax import lax
from jax.experimental import pallas as pl
from jax.experimental.pallas import tpu as pltpu
from jax.sharding import PartitionSpec as P

BEADS, OWNERS, SPACES, CELL, AUX, STEPS = 32, 32, 4, 128, 4, 2
TIME_STEP, FREQ, LENGTH, STRENGTH = 0.5, 1.5, 2.0, 0.1
HALF = 0.5 * TIME_STEP
SCALE = math.sqrt(math.log2(math.e))
SHIFT = LENGTH * SCALE
F32, BF16 = jnp.float32, jnp.bfloat16
MESH = pl.DeviceIdType.MESH
HIGHEST = lax.Precision.HIGHEST
UNROLL = 16


def constants():
    j = np.arange(BEADS, dtype=np.float64)
    phase = 2.0 * np.pi * j[:, None] * j[None, :] / BEADS
    k = j[None, :]
    basis = np.where(k < BEADS // 2, np.sqrt(2.0 / BEADS) * np.cos(phase), np.sqrt(2.0 / BEADS) * np.sin(phase))
    basis = np.where(k == 0, np.sqrt(1.0 / BEADS), basis)
    basis = np.where(k == BEADS // 2, np.sqrt(1.0 / BEADS) * np.cos(np.pi * j[:, None]), basis)
    freq = 2.0 * FREQ * np.sin(np.pi * j / BEADS)
    safe = np.where(j == 0, 1.0, freq)
    sinc = np.where(j == 0, TIME_STEP, np.sin(TIME_STEP * freq) / safe)
    out = np.zeros((5, BEADS, CELL), np.float32)
    out[0, :, :BEADS] = basis.T
    out[1, :, :BEADS] = basis
    out[2] = np.cos(TIME_STEP * freq)[:, None]
    out[3] = sinc[:, None]
    out[4] = (freq * np.sin(TIME_STEP * freq))[:, None]
    return out


def split3(x):
    a = x.astype(BF16).astype(F32)
    r = x - a
    b = r.astype(BF16).astype(F32)
    return a, b, r - b


def rhs_of(y):
    a, b, c = split3(y)
    return jnp.concatenate([a, b, a, b, c, a], axis=0).astype(BF16)


def lhs_of(x):
    a, b, c = split3(x)
    return jnp.concatenate([a, a, b, b, a, c], axis=0).T.astype(BF16)


def cell_force(x, ys):
    rhs = [rhs_of(y) for y in ys]
    right = jnp.concatenate(rhs, axis=1)
    left = jnp.concatenate([r[:16] for r in rhs], axis=1)
    e = lax.dot_general(lhs_of(x), right, (((1,), (0,)), ((), ())), preferred_element_type=F32)
    w = jnp.exp2(e)
    hi = w.astype(BF16)
    lo = (w - hi.astype(F32)).astype(BF16)
    nt = (((1,), (1,)), ((), ()))
    o = lax.dot_general(left, hi, nt, preferred_element_type=F32)
    o = o + lax.dot_general(left, lo, nt, preferred_element_type=F32)
    s = o[:8] + o[8:]
    return (STRENGTH / SCALE) * (x * s[3:4] - s)


def put_points(ref, base, tiles, shift, center):
    n = tiles[0].shape[0]
    t = [tiles[0] + shift, tiles[1], tiles[2]] if shift else list(tiles)
    norm = -0.5 * (t[0] * t[0] + t[1] * t[1] + t[2] * t[2])
    one = jnp.ones_like(norm)
    t += [norm, one] if center else [one, norm]
    t += [jnp.zeros_like(norm)] * 3
    for r, v in enumerate(t):
        ref[pl.ds(base + r, n, stride=8), :] = v


def all_forces(px, pm, p0, pp, fb, after):
    def step(i, carry):
        for u in range(UNROLL):
            at = pl.multiple_of((i * UNROLL + u) * 8, 8)
            nxt = pl.multiple_of(at + after, 8)
            ys = [pm[pl.ds(at, 8), :], p0[pl.ds(at, 8), :], pp[pl.ds(nxt, 8), :]]
            fb[pl.ds(at, 8), :] = cell_force(px[pl.ds(at, 8), :], ys)
        return carry

    lax.fori_loop(0, 64 // UNROLL, step, 0)


TILES = [(c, h) for c in range(3) for h in range(2)]


def mm(a, b):
    return jnp.dot(a, b, precision=HIGHEST, preferred_element_type=F32)


def exchange(me, send, recv, ssem, rsem):
    def copy(peer, slot):
        return pltpu.make_async_remote_copy(
            src_ref=send.at[pl.ds(pl.multiple_of(peer * 16, 16), 16)],
            dst_ref=recv.at[pl.ds(pl.multiple_of(slot * 16, 16), 16)],
            send_sem=ssem.at[peer],
            recv_sem=rsem.at[slot],
            device_id={"bead": peer},
            device_id_type=MESH,
        )

    def start(k, carry):
        copy(lax.rem(me + k, OWNERS), me).start()
        return carry

    lax.fori_loop(1, OWNERS, start, 0)
    own = pl.ds(pl.multiple_of(me * 16, 16), 16)
    recv[own, :] = send[own, :]

    def arrive(k, carry):
        peer = lax.rem(me + OWNERS - k, OWNERS)
        copy(peer, peer).wait_recv()
        return carry

    def sent(k, carry):
        copy(lax.rem(me + k, OWNERS), me).wait_send()
        return carry

    return (
        lambda: lax.fori_loop(1, OWNERS, arrive, 0),
        lambda: lax.fori_loop(1, OWNERS, sent, 0),
    )


def body(
    q_hbm, p_hbm, f_hbm, dr_hbm, mx_hbm, aux_hbm, noise_hbm, cst_hbm,
    q_out, p_out, f_out, aux_out,
    q, p, f, dr, mx, aux, noise, cst,
    send, recv, send2, recv2, edge, coef, u, u2, hs, hr,
    px, pm, p0, pp, fb,
    lsem, s1, r1, s2, r2, hssem, hrsem, essem, ersem,
):
    s, me = lax.axis_index("space"), lax.axis_index("bead")
    loads = [
        pltpu.make_async_copy(a, b, lsem.at[i])
        for i, (a, b) in enumerate(
            [(q_hbm, q), (p_hbm, p), (f_hbm, f), (dr_hbm, dr), (mx_hbm, mx), (aux_hbm, aux), (noise_hbm, noise), (cst_hbm, cst)]
        )
    ]
    for c in loads:
        c.start()
    barrier = pltpu.get_barrier_semaphore()
    up, down = lax.rem(s + 1, SPACES), lax.rem(s + SPACES - 1, SPACES)

    def greet(k, carry):
        pl.semaphore_signal(barrier, inc=1, device_id={"bead": lax.rem(me + k, OWNERS)}, device_id_type=MESH)
        return carry

    lax.fori_loop(1, OWNERS, greet, 0)
    for side in (up, down):
        pl.semaphore_signal(barrier, inc=1, device_id={"space": side}, device_id_type=MESH)
        pl.semaphore_signal(barrier, inc=1, device_id={"space": side, "bead": OWNERS - 1 - me}, device_id_type=MESH)

    for c in loads[:3]:
        c.wait()
    for h in range(2):
        for c in range(3):
            rows = pl.ds(h * 32, 32)
            send[pl.ds(h * 4 + c, 32, stride=16), :] = q[c, rows, :]
            send[pl.ds(8 + h * 4 + c, 32, stride=16), :] = p[c, rows, :] + HALF * f[c, rows, :]
    pl.semaphore_wait(barrier, OWNERS - 1 + 4)
    arrived, sent = exchange(me, send, recv, s1, r1)

    for c in loads[3:]:
        c.wait()
    for m, ref in enumerate((dr, mx)):
        for a in range(5):
            cols = ref[a].T
            for b in range(5):
                coef[m, a, b] = jnp.broadcast_to(cols[:, b : b + 1], (BEADS, CELL))
    for t, (c, h) in enumerate(TILES):
        lanes = pl.ds(t * CELL, CELL)
        state = [aux[pl.ds(c * 8 + h * 4 + a, 32, stride=24), :] for a in range(AUX)]
        kick = [[noise[st, b, c, :, pl.ds(h * CELL, CELL)] for b in range(5)] for st in range(STEPS)]
        for a in range(5):
            total = coef[1, a, 0] * kick[0][0]
            later = coef[1, a, 0] * kick[1][0]
            for b in range(1, 5):
                total = total + coef[1, a, b] * kick[0][b]
                later = later + coef[1, a, b] * kick[1][b]
            for b in range(AUX):
                total = total + coef[0, a, b + 1] * state[b]
            u[a, :, lanes] = total
            u2[a, :, lanes] = later

    arrived()
    fwd, inv = cst[0][:, :BEADS], cst[1][:, :BEADS]
    wide = lambda v: jnp.concatenate([v] * 6, axis=1)
    cosine, sinc, wsin = wide(cst[2]), wide(cst[3]), wide(cst[4])
    drift0 = [wide(coef[0, a, 0]) for a in range(5)]

    def free(qm, pm_, kick):
        z = drift0[0] * pm_ + kick[0]
        rest = [drift0[a] * pm_ + kick[a] for a in range(1, 5)]
        return qm * cosine + sinc * z, z * cosine - wsin * qm, rest

    qm = mm(fwd, jnp.concatenate([recv[pl.ds(h * 4 + c, 32, stride=16), :] for c, h in TILES], axis=1))
    pmode = mm(fwd, jnp.concatenate([recv[pl.ds(8 + h * 4 + c, 32, stride=16), :] for c, h in TILES], axis=1))
    qm, pmode, state = free(qm, pmode, u)
    points = mm(inv, qm) * SCALE
    tile = lambda v, c, h: v[:, (2 * c + h) * CELL : (2 * c + h + 1) * CELL]
    for h in range(2):
        for c in range(3):
            hs[h, c] = tile(points, c, h)

    halo = []
    for h in range(2):
        mine = s * 64 + h * 32 + me
        for side, step in ((0, 1), (1, 255)):
            there = lax.rem(mine + step, 256)
            slot = lax.rem(there // 32, 2)
            halo.append(
                pltpu.make_async_remote_copy(
                    src_ref=hs.at[h],
                    dst_ref=hr.at[side, slot],
                    send_sem=hssem.at[side, h],
                    recv_sem=hrsem.at[side, slot],
                    device_id={"space": there // 64, "bead": lax.rem(there, 32)},
                    device_id_type=MESH,
                )
            )
    for c in halo:
        c.start()
    for h in range(2):
        mine = [tile(points, c, h) for c in range(3)]
        put_points(px, h * 256, mine, 0.0, True)
        put_points(p0, h * 256, mine, 0.0, False)
    for a in range(5):
        total = u2[a]
        for b in range(AUX):
            total = total + wide(coef[0, a, b + 1]) * state[b]
        u2[a] = total
    for side, (ref, shift) in enumerate(((pm, -SHIFT), (pp, SHIFT))):
        for h in range(2):
            pltpu.make_async_remote_copy(
                src_ref=hs.at[h], dst_ref=hr.at[side, h], send_sem=hssem.at[side, h], recv_sem=hrsem.at[side, h],
                device_id={"space": up}, device_id_type=MESH,
            ).wait_recv()
            put_points(ref, h * 256, [hr[side, h, c] for c in range(3)], shift, False)
    all_forces(px, pm, p0, pp, fb, 0)
    force = jnp.concatenate([fb[pl.ds(h * 256 + c, 32, stride=8), :] for c, h in TILES], axis=1)
    pmode = pmode + 2.0 * HALF * mm(fwd, force)
    qm, pmode, state = free(qm, pmode, u2)
    qb, pb = mm(inv, qm), mm(inv, pmode)
    for c, h in TILES:
        send2[pl.ds(h * 4 + c, 32, stride=16), :] = tile(qb, c, h)
        send2[pl.ds(8 + h * 4 + c, 32, stride=16), :] = tile(pb, c, h)
    arrived2, sent2 = exchange(me, send2, recv2, s2, r2)
    for c, h in TILES:
        for a in range(AUX):
            aux_out[pl.ds(c * 8 + h * 4 + a, 32, stride=24), :] = tile(state[a], c, h)
    for c in halo:
        c.wait_send()
    sent()
    arrived2()
    edges = [
        pltpu.make_async_remote_copy(
            src_ref=recv2.at[pl.ds(src * 16, 8)],
            dst_ref=edge.at[pl.ds(side * 8, 8)],
            send_sem=essem.at[side],
            recv_sem=ersem.at[side],
            device_id={"space": where},
            device_id_type=MESH,
        )
        for side, (src, where) in enumerate(((OWNERS - 1, up), (0, down)))
    ]
    for c in edges:
        c.start()
    for h in range(2):
        tiles = []
        for c in range(3):
            t = recv2[pl.ds(h * 4 + c, 32, stride=16), :]
            q_out[c, pl.ds(h * 32, 32), :] = t
            tiles.append(t * SCALE)
        put_points(px, h * 256, tiles, 0.0, True)
        put_points(p0, h * 256, tiles, 0.0, False)
        put_points(pm, h * 256 + 8, tiles, -SHIFT, False)
        put_points(pp, h * 256, tiles, SHIFT, False)
    for c in edges:
        c.wait_recv()
    put_points(pm, 0, [edge[4 + c : 5 + c, :] * SCALE for c in range(3)], -SHIFT, False)
    put_points(pp, 512, [edge[8 + c : 9 + c, :] * SCALE for c in range(3)], SHIFT, False)
    all_forces(px, pm, p0, pp, fb, 8)
    for h in range(2):
        rows = pl.ds(h * 32, 32)
        for c in range(3):
            force = fb[pl.ds(h * 256 + c, 32, stride=8), :]
            f_out[c, rows, :] = force
            p_out[c, rows, :] = recv2[pl.ds(8 + h * 4 + c, 32, stride=16), :] + HALF * force
    for c in edges:
        c.wait_send()
    sent2()


def on_device(positions, momenta, forces, gle_drift, gle_noise_mix, aux_momenta, noise):
    cells = lambda v: v.reshape(3, 64, CELL)
    modes_last = lambda v: jnp.transpose(v, (1, 2, 0))
    aux = jnp.transpose(aux_momenta.reshape(BEADS, AUX, 3, 2, CELL), (0, 2, 3, 1, 4)).reshape(768, CELL)
    kicks = jnp.transpose(noise, (0, 2, 3, 1, 4))
    big = jax.ShapeDtypeStruct((3, 64, CELL), F32)
    vm = lambda *shape: pltpu.VMEM(shape, F32)
    dma = lambda *shape: pltpu.SemaphoreType.DMA(shape)
    any_, vmem = pl.BlockSpec(memory_space=pl.ANY), pl.BlockSpec(memory_space=pltpu.VMEM)
    q, p, f, a = pl.pallas_call(
        body,
        out_shape=(big, big, big, jax.ShapeDtypeStruct((768, CELL), F32)),
        in_specs=[any_] * 8,
        out_specs=(vmem,) * 4,
        scratch_shapes=[
            vm(3, 64, CELL), vm(3, 64, CELL), vm(3, 64, CELL), vm(5, 5, BEADS), vm(5, 5, BEADS),
            vm(768, CELL), vm(2, 5, 3, BEADS, 256), vm(5, BEADS, CELL),
            vm(512, CELL), vm(512, CELL), vm(512, CELL), vm(512, CELL), vm(16, CELL),
            vm(2, 5, 5, BEADS, CELL), vm(5, BEADS, 768), vm(5, BEADS, 768),
            vm(2, 3, BEADS, CELL), vm(2, 2, 3, BEADS, CELL),
            *([vm(520, CELL)] * 5),
            dma(8), dma(OWNERS), dma(OWNERS), dma(OWNERS), dma(OWNERS), dma(2, 2), dma(2, 2), dma(2), dma(2),
        ],
        compiler_params=pltpu.CompilerParams(collective_id=0, has_side_effects=True),
    )(cells(positions), cells(momenta), cells(forces), modes_last(gle_drift), modes_last(gle_noise_mix), aux, kicks, jnp.asarray(constants()))
    aux_new = jnp.transpose(a.reshape(BEADS, 3, 2, AUX, CELL), (0, 3, 1, 2, 4)).reshape(BEADS, AUX, 3, 256)
    back = lambda v: v.reshape(1, 3, 8192)
    return back(q), back(p), back(f), aux_new


def solution(mesh):
    wide = P("bead", None, "space")
    aux = P(None, None, None, ("space", "bead"))
    noise = P(None, None, None, None, ("space", "bead"))
    return jax.shard_map(
        on_device, mesh=mesh, in_specs=(wide, wide, wide, P(), P(), aux, noise),
        out_specs=(wide, wide, wide, aux), check_vma=False,
    )
```

profile of v0, /device:TPU:1, one launch (start us, length us, event | category | flops | bytes accessed | tf_op | source)
XLA Modules:
  0.0 61.4 jit_solution(11421419362240195219)
XLA Ops:
  0.6 55.3 %shard_map.111 = (f32[3,64,128]{2,1,0:T(8,128)}, f32[3,64,128]{2,1,0:T(8,128)}, f32[3,64,128]{2,1,0:T(8,128)}, f32[768,128]{1,0:T(8,128)}) custom-call(f32[3,64,128]{2,1,0:T(8,128)} %bitcast.22, f32[3,64,128]{2,1,0:T(8,128)} %bitcast.23, f32[3,64,128]{2,1,0:T(8,128)} %bitcast.24, f32[5,5,32]{2,1,0:T(8,128)} %bitcast.28, f32[5,5,32]{2,1,0:T(8,128)} %bitcast.29, ...), custom_call_target="tpu_custom_call" | custom-call | tf_op jit(solution)/shard_map/pallas_call | solution.py:316
  55.9 0.0 copy-start
  56.0 1.6 %copy.26 = f32[1,3,8192]{2,0,1:T(1,128)} copy(f32[1,3,8192]{2,0,1:T(1,128)} %bitcast.27) | data formatting | bytes 196608
  57.5 1.5 %copy.27 = f32[1,3,8192]{2,0,1:T(1,128)} copy(f32[1,3,8192]{2,0,1:T(1,128)} %bitcast.26) | data formatting | bytes 196608
  59.1 1.5 %copy.28 = f32[1,3,8192]{2,0,1:T(1,128)} copy(f32[1,3,8192]{2,0,1:T(1,128)} %bitcast.25) | data formatting | bytes 196608
  60.6 0.0 copy-done
  60.6 0.7 %copy.29 = f32[32,4,3,256]{3,1,2,0:T(4,128)} copy(f32[32,4,3,256]{3,1,2,0:T(4,128)S(1)} %bitcast.21) | data formatting | bytes 786432
Async XLA Ops:
  55.9 4.7 %copy-start = (f32[768,128]{1,0:T(8,128)S(1)}, f32[768,128]{1,0:T(8,128)}, u32[]{:S(2)}) copy-start(f32[768,128]{1,0:T(8,128)} %get-tuple-element.11) | copy-start | bytes 1179652
where the time goes:
time: 61.6 us; the launch traced here: 61.4 us
  Pallas kernels  55.3 us (90%)
  local copies, waits for them, and re-layouts  5.42 us (9%)
  between operations  0.65 us (1%)
    pallas_call x1, Pallas kernels, on_device(): pl.pallas_call(body, out_shape=(big, big, big, jax.ShapeDtypeStruct((768,...  55.3 us
    unnamed x6, local copies, waits for them, and re-layouts  5.42 us

commit v1 on v0

--- a/solution.py
+++ b/solution.py
@@ -16,7 +16,7 @@
 F32, BF16 = jnp.float32, jnp.bfloat16
 MESH = pl.DeviceIdType.MESH
 HIGHEST = lax.Precision.HIGHEST
-UNROLL = 16
+AHEAD = 4
 
 
 def constants():
@@ -55,19 +55,31 @@
     return jnp.concatenate([a, a, b, b, a, c], axis=0).T.astype(BF16)
 
 
-def cell_force(x, ys):
+def exponents(x, ys):
     rhs = [rhs_of(y) for y in ys]
+    left = jnp.concatenate([r[:16] for r in rhs for _ in range(2)], axis=1)
     right = jnp.concatenate(rhs, axis=1)
-    left = jnp.concatenate([r[:16] for r in rhs], axis=1)
-    e = lax.dot_general(lhs_of(x), right, (((1,), (0,)), ((), ())), preferred_element_type=F32)
-    w = jnp.exp2(e)
-    hi = w.astype(BF16)
-    lo = (w - hi.astype(F32)).astype(BF16)
-    nt = (((1,), (1,)), ((), ()))
-    o = lax.dot_general(left, hi, nt, preferred_element_type=F32)
-    o = o + lax.dot_general(left, lo, nt, preferred_element_type=F32)
-    s = o[:8] + o[8:]
-    return (STRENGTH / SCALE) * (x * s[3:4] - s)
+    return lax.dot_general(lhs_of(x), right, (((1,), (0,)), ((), ())), preferred_element_type=F32), left
+
+
+def pulls(e, left):
+    parts = []
+    for k in range(e.shape[1] // CELL):
+        w = jnp.exp2(e[:, k * CELL : (k + 1) * CELL])
+        hi = w.astype(BF16)
+        parts += [hi, (w - hi.astype(F32)).astype(BF16)]
+    w = jnp.concatenate(parts, axis=1)
+    o = lax.dot_general(left, w, (((1,), (1,)), ((), ())), preferred_element_type=F32)
+    return o[:8] + o[8:]
+
+
+def pipelined(cells, first, second):
+    todo = []
+    for i in range(len(cells) + AHEAD):
+        if i < len(cells):
+            todo.append(first(cells[i]))
+        if i >= AHEAD:
+            second(cells[i - AHEAD], *todo[i - AHEAD])
 
 
 def put_points(ref, base, tiles, shift, center):
@@ -81,16 +93,33 @@
         ref[pl.ds(base + r, n, stride=8), :] = v
 
 
-def all_forces(px, pm, p0, pp, fb, after):
-    def step(i, carry):
-        for u in range(UNROLL):
-            at = pl.multiple_of((i * UNROLL + u) * 8, 8)
-            nxt = pl.multiple_of(at + after, 8)
-            ys = [pm[pl.ds(at, 8), :], p0[pl.ds(at, 8), :], pp[pl.ds(nxt, 8), :]]
-            fb[pl.ds(at, 8), :] = cell_force(px[pl.ds(at, 8), :], ys)
-        return carry
-
-    lax.fori_loop(0, 64 // UNROLL, step, 0)
+def at(c):
+    return pl.ds(c * 8, 8)
+
+
+def force_of(x, s):
+    return (STRENGTH / SCALE) * (x * s[3:4] - s)
+
+
+def own_cells(px, p0, fb):
+    def second(c, e, left):
+        fb[at(c), :] = pulls(e, left)
+
+    pipelined(range(64), lambda c: exponents(px[at(c), :], [p0[at(c), :]]), second)
+
+
+def next_cells(px, pm, pp, fb):
+    def second(c, e, left):
+        fb[at(c), :] = force_of(px[at(c), :], fb[at(c), :] + pulls(e, left))
+
+    pipelined(range(64), lambda c: exponents(px[at(c), :], [pm[at(c), :], pp[at(c), :]]), second)
+
+
+def three_cells(cells, px, pm, p0, pp, fb):
+    def second(c, e, left):
+        fb[at(c), :] = force_of(px[at(c), :], pulls(e, left))
+
+    pipelined(cells, lambda c: exponents(px[at(c), :], [pm[at(c), :], p0[at(c), :], pp[at(c + 1), :]]), second)
 
 
 TILES = [(c, h) for c in range(3) for h in range(2)]
@@ -119,17 +148,26 @@
     own = pl.ds(pl.multiple_of(me * 16, 16), 16)
     recv[own, :] = send[own, :]
 
-    def arrive(k, carry):
-        peer = lax.rem(me + OWNERS - k, OWNERS)
-        copy(peer, peer).wait_recv()
+    def wait(peer):
+        @pl.when(peer != me)
+        def _():
+            copy(peer, peer).wait_recv()
+
+    def arrive(peer, carry):
+        wait(peer)
         return carry
 
     def sent(k, carry):
         copy(lax.rem(me + k, OWNERS), me).wait_send()
         return carry
 
+    def ends():
+        wait(OWNERS - 1)
+        wait(0)
+
     return (
-        lambda: lax.fori_loop(1, OWNERS, arrive, 0),
+        ends,
+        lambda: lax.fori_loop(1, OWNERS - 1, arrive, 0),
         lambda: lax.fori_loop(1, OWNERS, sent, 0),
     )
 
@@ -161,7 +199,13 @@
     lax.fori_loop(1, OWNERS, greet, 0)
     for side in (up, down):
         pl.semaphore_signal(barrier, inc=1, device_id={"space": side}, device_id_type=MESH)
-        pl.semaphore_signal(barrier, inc=1, device_id={"space": side, "bead": OWNERS - 1 - me}, device_id_type=MESH)
+
+    first, last = me == 0, me == OWNERS - 1
+
+    @pl.when(jnp.logical_or(first, last))
+    def _():
+        there, bead = jnp.where(first, down, up), OWNERS - 1 - me
+        pl.semaphore_signal(barrier, inc=1, device_id={"space": there, "bead": bead}, device_id_type=MESH)
 
     for c in loads[:3]:
         c.wait()
@@ -170,8 +214,8 @@
             rows = pl.ds(h * 32, 32)
             send[pl.ds(h * 4 + c, 32, stride=16), :] = q[c, rows, :]
             send[pl.ds(8 + h * 4 + c, 32, stride=16), :] = p[c, rows, :] + HALF * f[c, rows, :]
-    pl.semaphore_wait(barrier, OWNERS - 1 + 4)
-    arrived, sent = exchange(me, send, recv, s1, r1)
+    pl.semaphore_wait(barrier, OWNERS - 1 + 2 + jnp.where(jnp.logical_or(first, last), 1, 0))
+    ends, arrived, sent = exchange(me, send, recv, s1, r1)
 
     for c in loads[3:]:
         c.wait()
@@ -195,6 +239,7 @@
             u[a, :, lanes] = total
             u2[a, :, lanes] = later
 
+    ends()
     arrived()
     fwd, inv = cst[0][:, :BEADS], cst[1][:, :BEADS]
     wide = lambda v: jnp.concatenate([v] * 6, axis=1)
@@ -242,6 +287,7 @@
         for b in range(AUX):
             total = total + wide(coef[0, a, b + 1]) * state[b]
         u2[a] = total
+    own_cells(px, p0, fb)
     for side, (ref, shift) in enumerate(((pm, -SHIFT), (pp, SHIFT))):
         for h in range(2):
             pltpu.make_async_remote_copy(
@@ -249,7 +295,7 @@
                 device_id={"space": up}, device_id_type=MESH,
             ).wait_recv()
             put_points(ref, h * 256, [hr[side, h, c] for c in range(3)], shift, False)
-    all_forces(px, pm, p0, pp, fb, 0)
+    next_cells(px, pm, pp, fb)
     force = jnp.concatenate([fb[pl.ds(h * 256 + c, 32, stride=8), :] for c, h in TILES], axis=1)
     pmode = pmode + 2.0 * HALF * mm(fwd, force)
     qm, pmode, state = free(qm, pmode, u2)
@@ -257,14 +303,14 @@
     for c, h in TILES:
         send2[pl.ds(h * 4 + c, 32, stride=16), :] = tile(qb, c, h)
         send2[pl.ds(8 + h * 4 + c, 32, stride=16), :] = tile(pb, c, h)
-    arrived2, sent2 = exchange(me, send2, recv2, s2, r2)
+    ends2, arrived2, sent2 = exchange(me, send2, recv2, s2, r2)
     for c, h in TILES:
         for a in range(AUX):
             aux_out[pl.ds(c * 8 + h * 4 + a, 32, stride=24), :] = tile(state[a], c, h)
     for c in halo:
         c.wait_send()
     sent()
-    arrived2()
+    ends2()
     edges = [
         pltpu.make_async_remote_copy(
             src_ref=recv2.at[pl.ds(src * 16, 8)],
@@ -278,6 +324,7 @@
     ]
     for c in edges:
         c.start()
+    arrived2()
     for h in range(2):
         tiles = []
         for c in range(3):
@@ -288,11 +335,12 @@
         put_points(p0, h * 256, tiles, 0.0, False)
         put_points(pm, h * 256 + 8, tiles, -SHIFT, False)
         put_points(pp, h * 256, tiles, SHIFT, False)
+    three_cells(range(1, 63), px, pm, p0, pp, fb)
     for c in edges:
         c.wait_recv()
     put_points(pm, 0, [edge[4 + c : 5 + c, :] * SCALE for c in range(3)], -SHIFT, False)
     put_points(pp, 512, [edge[8 + c : 9 + c, :] * SCALE for c in range(3)], SHIFT, False)
-    all_forces(px, pm, p0, pp, fb, 8)
+    three_cells((0, 63), px, pm, p0, pp, fb)
     for h in range(2):
         rows = pl.ds(h * 32, 32)
         for c in range(3):
@@ -302,6 +350,14 @@
     for c in edges:
         c.wait_send()
     sent2()
+
+
+def hand_over(*refs):
+    copies = [pltpu.make_async_copy(refs[i], refs[4 + i], refs[8].at[i]) for i in range(4)]
+    for c in copies:
+        c.start()
+    for c in copies:
+        c.wait()
 
 
 def on_device(positions, momenta, forces, gle_drift, gle_noise_mix, aux_momenta, noise):
@@ -313,9 +369,10 @@
     vm = lambda *shape: pltpu.VMEM(shape, F32)
     dma = lambda *shape: pltpu.SemaphoreType.DMA(shape)
     any_, vmem = pl.BlockSpec(memory_space=pl.ANY), pl.BlockSpec(memory_space=pltpu.VMEM)
-    q, p, f, a = pl.pallas_call(
+    shapes = ((3, 64, CELL),) * 3 + ((768, CELL),)
+    results = pl.pallas_call(
         body,
-        out_shape=(big, big, big, jax.ShapeDtypeStruct((768, CELL), F32)),
+        out_shape=tuple(pltpu.VMEM(x, F32) for x in shapes),
         in_specs=[any_] * 8,
         out_specs=(vmem,) * 4,
         scratch_shapes=[
@@ -329,6 +386,13 @@
         ],
         compiler_params=pltpu.CompilerParams(collective_id=0, has_side_effects=True),
     )(cells(positions), cells(momenta), cells(forces), modes_last(gle_drift), modes_last(gle_noise_mix), aux, kicks, jnp.asarray(constants()))
+    q, p, f, a = pl.pallas_call(
+        hand_over,
+        out_shape=tuple(jax.ShapeDtypeStruct(x, F32) for x in shapes),
+        in_specs=[any_] * 4,
+        out_specs=(any_,) * 4,
+        scratch_shapes=[dma(4)],
+    )(*[pltpu.with_memory_space_constraint(x, pltpu.VMEM) for x in results])
     aux_new = jnp.transpose(a.reshape(BEADS, 3, 2, AUX, CELL), (0, 3, 1, 2, 4)).reshape(BEADS, AUX, 3, 256)
     back = lambda v: v.reshape(1, 3, 8192)
     return back(q), back(p), back(f), aux_new

time: 61.6 us -> 38.3 us (0.62)
  Pallas kernels: 55.3 us -> 37 us
  local copies, waits for them, and re-layouts: 5.42 us -> 0 us
    pallas_call x1 -> x2, Pallas kernels: 55.3 us -> 37 us  [the longest x1 36.1 us: on_device(): pl.pallas_call(body, out_shape=tuple((pltpu.VMEM(x, F32) for x in shapes)...]
    unnamed x6 -> x0, local copies, waits for them, and re-layouts: 5.42 us -> none
where the time goes in v1:
time: 38.3 us; the launch traced here: 37.6 us
  Pallas kernels  37 us (97%)
  between operations  0.64 us (2%)
    pallas_call x1, Pallas kernels, on_device(): pl.pallas_call(body, out_shape=tuple((pltpu.VMEM(x, F32) for x in shapes)...  36.1 us
    pallas_call x1, Pallas kernels, on_device(): pl.pallas_call(hand_over, out_shape=tuple((jax.ShapeDtypeStruct(x, F32) f...  0.88 us

profile of v1, /device:TPU:1, one launch (start us, length us, event | category | flops | bytes accessed | tf_op | source)
XLA Modules:
  0.0 37.6 jit_solution(18059165960323155172)
XLA Ops:
  0.6 36.1 %shard_map.111 = (f32[3,64,128]{2,1,0:T(8,128)S(1)}, f32[3,64,128]{2,1,0:T(8,128)S(1)}, f32[3,64,128]{2,1,0:T(8,128)S(1)}, f32[768,128]{1,0:T(8,128)S(1)}) custom-call(f32[3,64,128]{2,1,0:T(8,128)} %bitcast.21, f32[3,64,128]{2,1,0:T(8,128)} %bitcast.22, f32[3,64,128]{2,1,0:T(8,128)} %bitcast.23, f32[5,5,32]{2,1,0:T(8,128)} %bitcast.24, ...), custom_call_target="tpu_custom_call" | custom-call | tf_op jit(solution)/shard_map/pallas_call | solution.py:373
  36.8 0.9 %shard_map.112 = (f32[3,64,128]{2,1,0:T(8,128)}, f32[3,64,128]{2,1,0:T(8,128)}, f32[3,64,128]{2,1,0:T(8,128)}, f32[768,128]{1,0:T(8,128)}) custom-call(f32[3,64,128]{2,1,0:T(8,128)S(1)} %get-tuple-element.12.refs_0_, f32[3,64,128]{2,1,0:T(8,128)S(1)} %get-tuple-element.13.refs_1_, f32[3,64,128]{2,1,0:T(8,128)S(1)} %get-tuple-element.14.refs_2_, ...), custom_call_target="tpu_custom_call" | custom-call | tf_op jit(solution)/shard_map/pallas_call | solution.py:389

commit v2 on v1

v2 whole, which is shorter than its diff:
```python
import math

import jax
import jax.numpy as jnp
import numpy as np
from jax import lax
from jax.experimental import pallas as pl
from jax.experimental.pallas import tpu as pltpu
from jax.sharding import PartitionSpec as P

BEADS, OWNERS, SPACES, CELL, AUX, STEPS = 32, 32, 4, 128, 4, 2
TIME_STEP, FREQ, LENGTH, STRENGTH = 0.5, 1.5, 2.0, 0.1
HALF = 0.5 * TIME_STEP
SCALE = math.sqrt(math.log2(math.e))
SHIFT = LENGTH * SCALE
F32, BF16 = jnp.float32, jnp.bfloat16
MESH = pl.DeviceIdType.MESH
HIGHEST = lax.Precision.HIGHEST
AHEAD = 1
CHUNKS = 1
PART = BEADS // CHUNKS
ORDER1, ORDER2 = (2, 1, 3, 0), (0, 1, 3, 2)


def constants():
    j = np.arange(BEADS, dtype=np.float64)
    phase = 2.0 * np.pi * j[:, None] * j[None, :] / BEADS
    k = j[None, :]
    basis = np.where(k < BEADS // 2, np.sqrt(2.0 / BEADS) * np.cos(phase), np.sqrt(2.0 / BEADS) * np.sin(phase))
    basis = np.where(k == 0, np.sqrt(1.0 / BEADS), basis)
    basis = np.where(k == BEADS // 2, np.sqrt(1.0 / BEADS) * np.cos(np.pi * j[:, None]), basis)
    freq = 2.0 * FREQ * np.sin(np.pi * j / BEADS)
    safe = np.where(j == 0, 1.0, freq)
    sinc = np.where(j == 0, TIME_STEP, np.sin(TIME_STEP * freq) / safe)
    out = np.zeros((5, BEADS, CELL), np.float32)
    out[0, :, :BEADS] = basis.T
    out[1, :, :BEADS] = basis
    out[2] = np.cos(TIME_STEP * freq)[:, None]
    out[3] = sinc[:, None]
    out[4] = (freq * np.sin(TIME_STEP * freq))[:, None]
    return out


def split3(x):
    a = x.astype(BF16).astype(F32)
    r = x - a
    b = r.astype(BF16).astype(F32)
    return a, b, r - b


NN = (((1,), (0,)), ((), ()))


def exponents(xs, yss):
    none = jnp.zeros((48, CELL), BF16)
    sides = []
    for x in xs:
        a, b, c = split3(x)
        sides.append(jnp.concatenate([a, a, b, b, a, c], axis=0).astype(BF16))
    right = jnp.concatenate(
        [jnp.concatenate([sides[0], none], axis=1), jnp.concatenate([none, sides[1]], axis=1)], axis=0
    )
    rows, left = [], []
    for k in range(len(yss[0])):
        parts = [split3(ys[k]) for ys in yss]
        rows.append(jnp.concatenate([v for a, b, c in parts for v in (a, b, a, b, c, a)], axis=0).T.astype(BF16))
        left += [jnp.concatenate([v for a, b, _ in parts for v in (a, b)], axis=0).astype(BF16)] * 2
    e = lax.dot_general(jnp.concatenate(rows, axis=0), right, NN, preferred_element_type=F32)
    return e, jnp.concatenate(left, axis=1)


def pulls(e, left):
    parts = []
    for k in range(e.shape[0] // CELL):
        w = jnp.exp2(e[k * CELL : (k + 1) * CELL])
        hi = w.astype(BF16)
        parts += [hi, (w - hi.astype(F32)).astype(BF16)]
    o = lax.dot_general(left, jnp.concatenate(parts, axis=0), NN, preferred_element_type=F32)
    own = [o[16 * k : 16 * k + 16, CELL * k : CELL * k + CELL] for k in range(2)]
    return [v[:8] + v[8:] for v in own]


def pipelined(cells, x_of, ys_of, done):
    cells, todo = list(cells), []
    pairs = [cells[i : i + 2] for i in range(0, len(cells), 2)]
    for i in range(len(pairs) + AHEAD):
        if i < len(pairs):
            todo.append(exponents([x_of(c) for c in pairs[i]], [ys_of(c) for c in pairs[i]]))
        if i >= AHEAD:
            for c, v in zip(pairs[i - AHEAD], pulls(*todo[i - AHEAD])):
                done(c, v)


def put_fixed(px, others):
    one, zero = jnp.ones((65, CELL), F32), jnp.zeros((65, CELL), F32)
    for ref, row in [(px, 4)] + [(r, 3) for r in others]:
        for r in (row, 5, 6, 7):
            ref[pl.ds(r, 65, stride=8), :] = one if r == row else zero


def put_points(ref, base, tiles, shift, center):
    n = tiles[0].shape[0]
    t = [tiles[0] + shift, tiles[1], tiles[2]] if shift else list(tiles)
    norm = -0.5 * (t[0] * t[0] + t[1] * t[1] + t[2] * t[2])
    for r, v in enumerate(t):
        ref[pl.ds(base + r, n, stride=8), :] = v
    ref[pl.ds(base + (3 if center else 4), n, stride=8), :] = norm


def at(c):
    return pl.ds(pl.multiple_of(c * 8, 8), 8)


def force_of(x, s):
    return (STRENGTH / SCALE) * (x * s[3:4] - s)


def own_cells(px, p0, fb):
    def done(c, v):
        fb[at(c), :] = v

    pipelined(range(64), lambda c: px[at(c), :], lambda c: [p0[at(c), :]], done)


def next_cells(cells, px, pm, pp, fb):
    def done(c, v):
        fb[at(c), :] = force_of(px[at(c), :], fb[at(c), :] + v)

    pipelined(cells, lambda c: px[at(c), :], lambda c: [pm[at(c), :], pp[at(c), :]], done)


def three_cells(cells, px, pm, p0, pp, fb):
    def done(c, v):
        fb[at(c), :] = force_of(px[at(c), :], v)

    pipelined(cells, lambda c: px[at(c), :], lambda c: [pm[at(c), :], p0[at(c), :], pp[at(c + 1), :]], done)


TILES = [(c, h) for c in range(3) for h in range(2)]


def mm(a, b):
    return jnp.dot(a, b, precision=HIGHEST, preferred_element_type=F32)


def exchange(me, send, recv, ssem, rsem, first, rows, order):
    plane, place = me // 8, lax.rem(me, 8)

    def copy(peer, slot):
        return pltpu.make_async_remote_copy(
            src_ref=send.at[pl.ds(pl.multiple_of(peer * 16 + first, 8), rows)],
            dst_ref=recv.at[pl.ds(pl.multiple_of(slot * 16 + first, 8), rows)],
            send_sem=ssem.at[peer],
            recv_sem=rsem.at[slot],
            device_id={"bead": peer},
            device_id_type=MESH,
        )

    def each(step, act):
        base = lax.rem(plane + step, 4) * 8

        def one(k, carry):
            act(base + lax.rem(place + k, 8))
            return carry

        lax.fori_loop(0 if step else 1, 8, one, 0)

    for step in order:
        each(step, lambda peer: copy(peer, me).start())
    own = pl.ds(pl.multiple_of(me * 16 + first, 8), 8 * (1 + rows // 8))
    recv[own, :] = send[own, :]

    def arrived(step):
        each(step, lambda peer: copy(peer, peer).wait_recv())

    def sent():
        for step in order:
            each(step, lambda peer: copy(peer, me).wait_send())

    return arrived, sent


def body(
    q_hbm, p_hbm, f_hbm, dr_hbm, mx_hbm, aux_hbm, noise_hbm, cst_hbm,
    q_out, p_out, f_out, aux_out,
    q, p, f, dr, mx, aux, noise, cst,
    send, recv, send2, recv2, edge, coef, u, u2, hs, hr,
    px, pm, p0, pp, fb,
    lsem, s1, r1, s2, r2, s3, r3, hssem, hrsem, essem, ersem,
):
    s, me = lax.axis_index("space"), lax.axis_index("bead")
    loads = [
        pltpu.make_async_copy(a, b, lsem.at[i])
        for i, (a, b) in enumerate(
            [(q_hbm, q), (p_hbm, p), (f_hbm, f), (dr_hbm, dr), (mx_hbm, mx), (aux_hbm, aux), (noise_hbm, noise), (cst_hbm, cst)]
        )
    ]
    for c in loads:
        c.start()
    barrier = pltpu.get_barrier_semaphore()
    up, down = lax.rem(s + 1, SPACES), lax.rem(s + SPACES - 1, SPACES)

    def greet(k, carry):
        pl.semaphore_signal(barrier, inc=1, device_id={"bead": lax.rem(me + k, OWNERS)}, device_id_type=MESH)
        return carry

    lax.fori_loop(1, OWNERS, greet, 0)

    first, last = me == 0, me == OWNERS - 1

    @pl.when(jnp.logical_or(first, last))
    def _():
        there, bead = jnp.where(first, down, up), OWNERS - 1 - me
        pl.semaphore_signal(barrier, inc=1, device_id={"space": there, "bead": bead}, device_id_type=MESH)

    for c in loads[:3]:
        c.wait()
    for h in range(2):
        for c in range(3):
            rows = pl.ds(h * 32, 32)
            send[pl.ds(h * 3 + c, 32, stride=16), :] = q[c, rows, :]
            send[pl.ds(6 + h * 3 + c, 32, stride=16), :] = p[c, rows, :] + HALF * f[c, rows, :]
    put_fixed(px, (pm, p0, pp))
    pl.semaphore_wait(barrier, OWNERS - 1 + jnp.where(jnp.logical_or(first, last), 1, 0))
    arrived, sent = exchange(me, send, recv, s1, r1, 0, 12, ORDER1)

    for c in loads[3:]:
        c.wait()
    for m, ref in enumerate((dr, mx)):
        for a in range(5):
            cols = ref[a].T
            for b in range(5):
                coef[m, a, b] = jnp.broadcast_to(cols[:, b : b + 1], (BEADS, CELL))
    for t, (c, h) in enumerate(TILES):
        lanes = pl.ds(t * CELL, CELL)
        state = [aux[pl.ds(c * 8 + h * 4 + a, 32, stride=24), :] for a in range(AUX)]
        kick = [[noise[st, b, c, :, pl.ds(h * CELL, CELL)] for b in range(5)] for st in range(STEPS)]
        for a in range(5):
            total = coef[1, a, 0] * kick[0][0]
            later = coef[1, a, 0] * kick[1][0]
            for b in range(1, 5):
                total = total + coef[1, a, b] * kick[0][b]
                later = later + coef[1, a, b] * kick[1][b]
            for b in range(AUX):
                total = total + coef[0, a, b + 1] * state[b]
            u[a, :, lanes] = total
            u2[a, :, lanes] = later

    for step in range(4):
        arrived(step)
    fwd, inv = cst[0][:, :BEADS], cst[1][:, :BEADS]
    wide = lambda v: jnp.concatenate([v] * 6, axis=1)
    cosine, sinc, wsin = wide(cst[2]), wide(cst[3]), wide(cst[4])
    drift0 = [wide(coef[0, a, 0]) for a in range(5)]

    def free(qm, pm_, kick):
        z = drift0[0] * pm_ + kick[0]
        rest = [drift0[a] * pm_ + kick[a] for a in range(1, 5)]
        return qm * cosine + sinc * z, z * cosine - wsin * qm, rest

    qm = mm(fwd, jnp.concatenate([recv[pl.ds(h * 3 + c, 32, stride=16), :] for c, h in TILES], axis=1))
    pmode = mm(fwd, jnp.concatenate([recv[pl.ds(6 + h * 3 + c, 32, stride=16), :] for c, h in TILES], axis=1))
    qm, pmode, state = free(qm, pmode, u)
    points = mm(inv, qm) * SCALE
    tile = lambda v, c, h: v[:, (2 * c + h) * CELL : (2 * c + h + 1) * CELL]
    for h in range(2):
        for c in range(3):
            hs[h, c] = tile(points, c, h)

    halo = []
    for k in range(CHUNKS):
        beads = pl.ds(k * PART, PART)
        for h in range(2):
            mine = s * 64 + h * 32 + me
            for side, step in ((0, 1), (1, 255)):
                there = lax.rem(mine + step, 256)
                slot = lax.rem(there // 32, 2)
                halo.append(
                    pltpu.make_async_remote_copy(
                        src_ref=hs.at[h, :, beads],
                        dst_ref=hr.at[side, slot, :, beads],
                        send_sem=hssem.at[k, side, h],
                        recv_sem=hrsem.at[k, side, slot],
                        device_id={"space": there // 64, "bead": lax.rem(there, 32)},
                        device_id_type=MESH,
                    )
                )
    for c in halo:
        c.start()
    for h in range(2):
        mine = [tile(points, c, h) for c in range(3)]
        put_points(px, h * 256, mine, 0.0, True)
        put_points(p0, h * 256, mine, 0.0, False)
    for a in range(5):
        total = u2[a]
        for b in range(AUX):
            total = total + wide(coef[0, a, b + 1]) * state[b]
        u2[a] = total
    own_cells(px, p0, fb)
    for k in range(CHUNKS):
        beads = pl.ds(k * PART, PART)
        for side, (ref, shift) in enumerate(((pm, -SHIFT), (pp, SHIFT))):
            for h in range(2):
                pltpu.make_async_remote_copy(
                    src_ref=hs.at[h, :, beads], dst_ref=hr.at[side, h, :, beads],
                    send_sem=hssem.at[k, side, h], recv_sem=hrsem.at[k, side, h],
                    device_id={"space": up}, device_id_type=MESH,
                ).wait_recv()
                put_points(ref, h * 256 + k * PART * 8, [hr[side, h, c, beads, :] for c in range(3)], shift, False)
        next_cells([h * 32 + k * PART + i for h in range(2) for i in range(PART)], px, pm, pp, fb)
    force = jnp.concatenate([fb[pl.ds(h * 256 + c, 32, stride=8), :] for c, h in TILES], axis=1)
    pmode = pmode + 2.0 * HALF * mm(fwd, force)
    qm, pmode, state = free(qm, pmode, u2)
    qb = mm(inv, qm)
    for c, h in TILES:
        send2[pl.ds(h * 3 + c, 32, stride=16), :] = tile(qb, c, h)
    arrived2, sent2 = exchange(me, send2, recv2, s2, r2, 0, 6, ORDER2)

    def edge_copy(side, bead):
        return pltpu.make_async_remote_copy(
            src_ref=send2.at[pl.ds(pl.multiple_of(bead * 16, 16), 6)],
            dst_ref=edge.at[pl.ds(side * 8, 6)],
            send_sem=essem.at[bead],
            recv_sem=ersem.at[side],
            device_id={"space": (up, down)[side], "bead": bead},
            device_id_type=MESH,
        )

    def edge_owners(act):
        for side, owner in ((0, last), (1, first)):

            @pl.when(owner)
            def _():
                def one(k, carry):
                    act(edge_copy(side, lax.rem(me + k, OWNERS)))
                    return carry

                lax.fori_loop(0, OWNERS, one, 0)

    edge_owners(lambda copy: copy.start())
    pb = mm(inv, pmode)
    for c, h in TILES:
        send2[pl.ds(8 + h * 3 + c, 32, stride=16), :] = tile(pb, c, h)
    arrived3, sent3 = exchange(me, send2, recv2, s3, r3, 8, 6, ORDER2)
    for c, h in TILES:
        for a in range(AUX):
            aux_out[pl.ds(c * 8 + h * 4 + a, 32, stride=24), :] = tile(state[a], c, h)
    for c in halo:
        c.wait_send()
    sent()
    plane = me // 8
    for step in range(4):
        arrived2(step)
    for h in range(2):
        tiles = [recv2[pl.ds(h * 3 + c, 32, stride=16), :] * SCALE for c in range(3)]
        put_points(px, h * 256, tiles, 0.0, True)
        put_points(p0, h * 256, tiles, 0.0, False)
        put_points(pm, h * 256 + 8, tiles, -SHIFT, False)
        put_points(pp, h * 256, tiles, SHIFT, False)
    three_cells(range(1, 63), px, pm, p0, pp, fb)
    for side in range(2):
        edge_copy(side, 0).wait_recv()
    put_points(pm, 0, [edge[3 + c : 4 + c, :] * SCALE for c in range(3)], -SHIFT, False)
    put_points(pp, 512, [edge[8 + c : 9 + c, :] * SCALE for c in range(3)], SHIFT, False)
    three_cells((0, 63), px, pm, p0, pp, fb)
    for step in range(4):
        arrived3(step)
    for h in range(2):
        rows = pl.ds(h * 32, 32)
        for c in range(3):
            force = fb[pl.ds(h * 256 + c, 32, stride=8), :]
            f_out[c, rows, :] = force
            q_out[c, rows, :] = recv2[pl.ds(h * 3 + c, 32, stride=16), :]
            p_out[c, rows, :] = recv2[pl.ds(8 + h * 3 + c, 32, stride=16), :] + HALF * force
    edge_owners(lambda copy: copy.wait_send())
    sent2()
    sent3()


def hand_over(*refs):
    copies = [pltpu.make_async_copy(refs[i], refs[4 + i], refs[8].at[i]) for i in range(4)]
    for c in copies:
        c.start()
    for c in copies:
        c.wait()


def on_device(positions, momenta, forces, gle_drift, gle_noise_mix, aux_momenta, noise):
    cells = lambda v: v.reshape(3, 64, CELL)
    modes_last = lambda v: jnp.transpose(v, (1, 2, 0))
    aux = jnp.transpose(aux_momenta.reshape(BEADS, AUX, 3, 2, CELL), (0, 2, 3, 1, 4)).reshape(768, CELL)
    kicks = jnp.transpose(noise, (0, 2, 3, 1, 4))
    big = jax.ShapeDtypeStruct((3, 64, CELL), F32)
    vm = lambda *shape: pltpu.VMEM(shape, F32)
    dma = lambda *shape: pltpu.SemaphoreType.DMA(shape)
    any_, vmem = pl.BlockSpec(memory_space=pl.ANY), pl.BlockSpec(memory_space=pltpu.VMEM)
    shapes = ((3, 64, CELL),) * 3 + ((768, CELL),)
    results = pl.pallas_call(
        body,
        out_shape=tuple(pltpu.VMEM(x, F32) for x in shapes),
        in_specs=[any_] * 8,
        out_specs=(vmem,) * 4,
        scratch_shapes=[
            vm(3, 64, CELL), vm(3, 64, CELL), vm(3, 64, CELL), vm(5, 5, BEADS), vm(5, 5, BEADS),
            vm(768, CELL), vm(2, 5, 3, BEADS, 256), vm(5, BEADS, CELL),
            vm(512, CELL), vm(512, CELL), vm(512, CELL), vm(512, CELL), vm(16, CELL),
            vm(2, 5, 5, BEADS, CELL), vm(5, BEADS, 768), vm(5, BEADS, 768),
            vm(2, 3, BEADS, CELL), vm(2, 2, 3, BEADS, CELL),
            *([vm(520, CELL)] * 5),
            dma(8), *([dma(OWNERS)] * 6), dma(CHUNKS, 2, 2), dma(CHUNKS, 2, 2), dma(OWNERS), dma(2),
        ],
        compiler_params=pltpu.CompilerParams(collective_id=0, has_side_effects=True),
    )(cells(positions), cells(momenta), cells(forces), modes_last(gle_drift), modes_last(gle_noise_mix), aux, kicks, jnp.asarray(constants()))
    q, p, f, a = pl.pallas_call(
        hand_over,
        out_shape=tuple(jax.ShapeDtypeStruct(x, F32) for x in shapes),
        in_specs=[any_] * 4,
        out_specs=(any_,) * 4,
        scratch_shapes=[dma(4)],
    )(*[pltpu.with_memory_space_constraint(x, pltpu.VMEM) for x in results])
    aux_new = jnp.transpose(a.reshape(BEADS, 3, 2, AUX, CELL), (0, 3, 1, 2, 4)).reshape(BEADS, AUX, 3, 256)
    back = lambda v: v.reshape(1, 3, 8192)
    return back(q), back(p), back(f), aux_new


def solution(mesh):
    wide = P("bead", None, "space")
    aux = P(None, None, None, ("space", "bead"))
    noise = P(None, None, None, None, ("space", "bead"))
    return jax.shard_map(
        on_device, mesh=mesh, in_specs=(wide, wide, wide, P(), P(), aux, noise),
        out_specs=(wide, wide, wide, aux), check_vma=False,
    )
```

time: 38.3 us -> 36.7 us (0.958)
  Pallas kernels: 37 us -> 35.3 us
    pallas_call x1, Pallas kernels: 36.1 us -> 34.4 us  [on_device(): pl.pallas_call(body, out_shape=tuple((pltpu.VMEM(x, F32) for x in shapes)...]
where the time goes in v2:
time: 36.7 us; the launch traced here: 36 us
  Pallas kernels  35.3 us (96%)
  between operations  0.64 us (2%)
    pallas_call x1, Pallas kernels, on_device(): pl.pallas_call(body, out_shape=tuple((pltpu.VMEM(x, F32) for x in shapes)...  34.4 us
    pallas_call x1, Pallas kernels, on_device(): pl.pallas_call(hand_over, out_shape=tuple((jax.ShapeDtypeStruct(x, F32) f...  0.88 us

profile of v2, /device:TPU:1, one launch (start us, length us, event | category | flops | bytes accessed | tf_op | source)
XLA Modules:
  0.0 36.0 jit_solution(6417421244532311857)
XLA Ops:
  0.6 34.4 %shard_map.111 = (f32[3,64,128]{2,1,0:T(8,128)S(1)}, f32[3,64,128]{2,1,0:T(8,128)S(1)}, f32[3,64,128]{2,1,0:T(8,128)S(1)}, f32[768,128]{1,0:T(8,128)S(1)}) custom-call(f32[3,64,128]{2,1,0:T(8,128)} %bitcast.21, f32[3,64,128]{2,1,0:T(8,128)} %bitcast.22, f32[3,64,128]{2,1,0:T(8,128)} %bitcast.23, f32[5,5,32]{2,1,0:T(8,128)} %bitcast.24, ...), custom_call_target="tpu_custom_call" | custom-call | tf_op jit(solution)/shard_map/pallas_call | solution.py:398
  35.1 0.9 %shard_map.112 = (f32[3,64,128]{2,1,0:T(8,128)}, f32[3,64,128]{2,1,0:T(8,128)}, f32[3,64,128]{2,1,0:T(8,128)}, f32[768,128]{1,0:T(8,128)}) custom-call(f32[3,64,128]{2,1,0:T(8,128)S(1)} %get-tuple-element.12.refs_0_, f32[3,64,128]{2,1,0:T(8,128)S(1)} %get-tuple-element.13.refs_1_, f32[3,64,128]{2,1,0:T(8,128)S(1)} %get-tuple-element.14.refs_2_, ...), custom_call_target="tpu_custom_call" | custom-call | tf_op jit(solution)/shard_map/pallas_call | solution.py:414

commit v3 on v2

--- a/solution.py
+++ b/solution.py
@@ -19,7 +19,7 @@
 AHEAD = 1
 CHUNKS = 1
 PART = BEADS // CHUNKS
-ORDER1, ORDER2 = (2, 1, 3, 0), (0, 1, 3, 2)
+ORDER1, ORDER2 = (2, 1, 3, 0), (2, 1, 3, 0)
 
 
 def constants():
@@ -143,41 +143,29 @@
     return jnp.dot(a, b, precision=HIGHEST, preferred_element_type=F32)
 
 
+def take(sem, like, rows):
+    part = like.at[pl.ds(0, rows)]
+    pltpu.make_async_copy(part, part, sem).wait()
+
+
 def exchange(me, send, recv, ssem, rsem, first, rows, order):
     plane, place = me // 8, lax.rem(me, 8)
-
-    def copy(peer, slot):
-        return pltpu.make_async_remote_copy(
-            src_ref=send.at[pl.ds(pl.multiple_of(peer * 16 + first, 8), rows)],
-            dst_ref=recv.at[pl.ds(pl.multiple_of(slot * 16 + first, 8), rows)],
-            send_sem=ssem.at[peer],
-            recv_sem=rsem.at[slot],
-            device_id={"bead": peer},
-            device_id_type=MESH,
-        )
-
-    def each(step, act):
+    for step in order:
         base = lax.rem(plane + step, 4) * 8
-
-        def one(k, carry):
-            act(base + lax.rem(place + k, 8))
-            return carry
-
-        lax.fori_loop(0 if step else 1, 8, one, 0)
-
-    for step in order:
-        each(step, lambda peer: copy(peer, me).start())
+        for k in range(0 if step else 1, 8):
+            peer = base + lax.rem(place + k, 8)
+            pltpu.make_async_remote_copy(
+                src_ref=send.at[pl.ds(pl.multiple_of(peer * 16 + first, 8), rows)],
+                dst_ref=recv.at[pl.ds(pl.multiple_of(me * 16 + first, 8), rows)],
+                send_sem=ssem,
+                recv_sem=rsem,
+                device_id={"bead": peer},
+                device_id_type=MESH,
+            ).start()
     own = pl.ds(pl.multiple_of(me * 16 + first, 8), 8 * (1 + rows // 8))
     recv[own, :] = send[own, :]
-
-    def arrived(step):
-        each(step, lambda peer: copy(peer, peer).wait_recv())
-
-    def sent():
-        for step in order:
-            each(step, lambda peer: copy(peer, me).wait_send())
-
-    return arrived, sent
+    total = (OWNERS - 1) * rows
+    return (lambda: take(rsem, recv, total)), (lambda: take(ssem, send, total))
 
 
 def body(
@@ -186,7 +174,7 @@
     q, p, f, dr, mx, aux, noise, cst,
     send, recv, send2, recv2, edge, coef, u, u2, hs, hr,
     px, pm, p0, pp, fb,
-    lsem, s1, r1, s2, r2, s3, r3, hssem, hrsem, essem, ersem,
+    lsem, ssem, rsem, hssem, hrsem, essem, ersem,
 ):
     s, me = lax.axis_index("space"), lax.axis_index("bead")
     loads = [
@@ -200,11 +188,8 @@
     barrier = pltpu.get_barrier_semaphore()
     up, down = lax.rem(s + 1, SPACES), lax.rem(s + SPACES - 1, SPACES)
 
-    def greet(k, carry):
+    for k in range(1, OWNERS):
         pl.semaphore_signal(barrier, inc=1, device_id={"bead": lax.rem(me + k, OWNERS)}, device_id_type=MESH)
-        return carry
-
-    lax.fori_loop(1, OWNERS, greet, 0)
 
     first, last = me == 0, me == OWNERS - 1
 
@@ -222,7 +207,7 @@
             send[pl.ds(6 + h * 3 + c, 32, stride=16), :] = p[c, rows, :] + HALF * f[c, rows, :]
     put_fixed(px, (pm, p0, pp))
     pl.semaphore_wait(barrier, OWNERS - 1 + jnp.where(jnp.logical_or(first, last), 1, 0))
-    arrived, sent = exchange(me, send, recv, s1, r1, 0, 12, ORDER1)
+    arrived, sent = exchange(me, send, recv, ssem.at[0], rsem.at[0], 0, 12, ORDER1)
 
     for c in loads[3:]:
         c.wait()
@@ -246,8 +231,7 @@
             u[a, :, lanes] = total
             u2[a, :, lanes] = later
 
-    for step in range(4):
-        arrived(step)
+    arrived()
     fwd, inv = cst[0][:, :BEADS], cst[1][:, :BEADS]
     wide = lambda v: jnp.concatenate([v] * 6, axis=1)
     cosine, sinc, wsin = wide(cst[2]), wide(cst[3]), wide(cst[4])
@@ -314,13 +298,13 @@
     qb = mm(inv, qm)
     for c, h in TILES:
         send2[pl.ds(h * 3 + c, 32, stride=16), :] = tile(qb, c, h)
-    arrived2, sent2 = exchange(me, send2, recv2, s2, r2, 0, 6, ORDER2)
+    arrived2, sent2 = exchange(me, send2, recv2, ssem.at[1], rsem.at[1], 0, 6, ORDER2)
 
     def edge_copy(side, bead):
         return pltpu.make_async_remote_copy(
             src_ref=send2.at[pl.ds(pl.multiple_of(bead * 16, 16), 6)],
             dst_ref=edge.at[pl.ds(side * 8, 6)],
-            send_sem=essem.at[bead],
+            send_sem=essem.at[0],
             recv_sem=ersem.at[side],
             device_id={"space": (up, down)[side], "bead": bead},
             device_id_type=MESH,
@@ -341,16 +325,14 @@
     pb = mm(inv, pmode)
     for c, h in TILES:
         send2[pl.ds(8 + h * 3 + c, 32, stride=16), :] = tile(pb, c, h)
-    arrived3, sent3 = exchange(me, send2, recv2, s3, r3, 8, 6, ORDER2)
+    arrived3, sent3 = exchange(me, send2, recv2, ssem.at[2], rsem.at[2], 8, 6, ORDER2)
     for c, h in TILES:
         for a in range(AUX):
             aux_out[pl.ds(c * 8 + h * 4 + a, 32, stride=24), :] = tile(state[a], c, h)
     for c in halo:
         c.wait_send()
     sent()
-    plane = me // 8
-    for step in range(4):
-        arrived2(step)
+    arrived2()
     for h in range(2):
         tiles = [recv2[pl.ds(h * 3 + c, 32, stride=16), :] * SCALE for c in range(3)]
         put_points(px, h * 256, tiles, 0.0, True)
@@ -363,8 +345,7 @@
     put_points(pm, 0, [edge[3 + c : 4 + c, :] * SCALE for c in range(3)], -SHIFT, False)
     put_points(pp, 512, [edge[8 + c : 9 + c, :] * SCALE for c in range(3)], SHIFT, False)
     three_cells((0, 63), px, pm, p0, pp, fb)
-    for step in range(4):
-        arrived3(step)
+    arrived3()
     for h in range(2):
         rows = pl.ds(h * 32, 32)
         for c in range(3):
@@ -372,7 +353,12 @@
             f_out[c, rows, :] = force
             q_out[c, rows, :] = recv2[pl.ds(h * 3 + c, 32, stride=16), :]
             p_out[c, rows, :] = recv2[pl.ds(8 + h * 3 + c, 32, stride=16), :] + HALF * force
-    edge_owners(lambda copy: copy.wait_send())
+    for owner in (last, first):
+
+        @pl.when(owner)
+        def _():
+            take(essem.at[0], send2, OWNERS * 6)
+
     sent2()
     sent3()
 
@@ -407,7 +393,7 @@
             vm(2, 5, 5, BEADS, CELL), vm(5, BEADS, 768), vm(5, BEADS, 768),
             vm(2, 3, BEADS, CELL), vm(2, 2, 3, BEADS, CELL),
             *([vm(520, CELL)] * 5),
-            dma(8), *([dma(OWNERS)] * 6), dma(CHUNKS, 2, 2), dma(CHUNKS, 2, 2), dma(OWNERS), dma(2),
+            dma(8), dma(3), dma(3), dma(CHUNKS, 2, 2), dma(CHUNKS, 2, 2), dma(1), dma(2),
         ],
         compiler_params=pltpu.CompilerParams(collective_id=0, has_side_effects=True),
     )(cells(positions), cells(momenta), cells(forces), modes_last(gle_drift), modes_last(gle_noise_mix), aux, kicks, jnp.asarray(constants()))

time: 36.7 us -> 32.9 us (0.90); the launches traced: 36 us -> 32.7 us
  Pallas kernels: 35.3 us -> 32 us
    pallas_call x1, Pallas kernels: 34.4 us -> 31.2 us  [on_device(): pl.pallas_call(body, out_shape=tuple((pltpu.VMEM(x, F32) for x in shapes)...]
where the time goes in v3:
time: 32.9 us; the launch traced here: 32.7 us
  Pallas kernels  32 us (97%)
  between operations  0.64 us (2%)
    pallas_call x1, Pallas kernels, on_device(): pl.pallas_call(body, out_shape=tuple((pltpu.VMEM(x, F32) for x in shapes)...  31.2 us
    pallas_call x1, Pallas kernels, on_device(): pl.pallas_call(hand_over, out_shape=tuple((jax.ShapeDtypeStruct(x, F32) f...  0.88 us

profile of v3, /device:TPU:1, one launch (start us, length us, event | category | flops | bytes accessed | tf_op | source)
XLA Modules:
  0.0 32.7 jit_solution(5288021868431349526)
XLA Ops:
  0.6 31.2 %shard_map.111 = (f32[3,64,128]{2,1,0:T(8,128)S(1)}, f32[3,64,128]{2,1,0:T(8,128)S(1)}, f32[3,64,128]{2,1,0:T(8,128)S(1)}, f32[768,128]{1,0:T(8,128)S(1)}) custom-call(f32[3,64,128]{2,1,0:T(8,128)} %bitcast.21, f32[3,64,128]{2,1,0:T(8,128)} %bitcast.22, f32[3,64,128]{2,1,0:T(8,128)} %bitcast.23, f32[5,5,32]{2,1,0:T(8,128)} %bitcast.24, ...), custom_call_target="tpu_custom_call" | custom-call | tf_op jit(solution)/shard_map/pallas_call | solution.py:384
  31.8 0.9 %shard_map.112 = (f32[3,64,128]{2,1,0:T(8,128)}, f32[3,64,128]{2,1,0:T(8,128)}, f32[3,64,128]{2,1,0:T(8,128)}, f32[768,128]{1,0:T(8,128)}) custom-call(f32[3,64,128]{2,1,0:T(8,128)S(1)} %get-tuple-element.12.refs_0_, f32[3,64,128]{2,1,0:T(8,128)S(1)} %get-tuple-element.13.refs_1_, f32[3,64,128]{2,1,0:T(8,128)S(1)} %get-tuple-element.14.refs_2_, ...), custom_call_target="tpu_custom_call" | custom-call | tf_op jit(solution)/shard_map/pallas_call | solution.py:400

commit v4 on v3

--- a/solution.py
+++ b/solution.py
@@ -17,6 +17,7 @@
 MESH = pl.DeviceIdType.MESH
 HIGHEST = lax.Precision.HIGHEST
 AHEAD = 1
+STAGES = ((0,), (1, 3, 2))
 CHUNKS = 1
 PART = BEADS // CHUNKS
 ORDER1, ORDER2 = (2, 1, 3, 0), (2, 1, 3, 0)
@@ -148,7 +149,7 @@
     pltpu.make_async_copy(part, part, sem).wait()
 
 
-def exchange(me, send, recv, ssem, rsem, first, rows, order):
+def exchange(me, send, recv, ssem, rsem, first, rows, order, planes=None):
     plane, place = me // 8, lax.rem(me, 8)
     for step in order:
         base = lax.rem(plane + step, 4) * 8
@@ -158,7 +159,7 @@
                 src_ref=send.at[pl.ds(pl.multiple_of(peer * 16 + first, 8), rows)],
                 dst_ref=recv.at[pl.ds(pl.multiple_of(me * 16 + first, 8), rows)],
                 send_sem=ssem,
-                recv_sem=rsem,
+                recv_sem=rsem if planes is None else planes.at[plane],
                 device_id={"bead": peer},
                 device_id_type=MESH,
             ).start()
@@ -174,7 +175,7 @@
     q, p, f, dr, mx, aux, noise, cst,
     send, recv, send2, recv2, edge, coef, u, u2, hs, hr,
     px, pm, p0, pp, fb,
-    lsem, ssem, rsem, hssem, hrsem, essem, ersem,
+    lsem, ssem, rsem, psem, hssem, hrsem, essem, ersem,
 ):
     s, me = lax.axis_index("space"), lax.axis_index("bead")
     loads = [
@@ -298,7 +299,7 @@
     qb = mm(inv, qm)
     for c, h in TILES:
         send2[pl.ds(h * 3 + c, 32, stride=16), :] = tile(qb, c, h)
-    arrived2, sent2 = exchange(me, send2, recv2, ssem.at[1], rsem.at[1], 0, 6, ORDER2)
+    _, sent2 = exchange(me, send2, recv2, ssem.at[1], rsem.at[1], 0, 6, ORDER2, psem)
 
     def edge_copy(side, bead):
         return pltpu.make_async_remote_copy(
@@ -332,14 +333,23 @@
     for c in halo:
         c.wait_send()
     sent()
-    arrived2()
-    for h in range(2):
-        tiles = [recv2[pl.ds(h * 3 + c, 32, stride=16), :] * SCALE for c in range(3)]
-        put_points(px, h * 256, tiles, 0.0, True)
-        put_points(p0, h * 256, tiles, 0.0, False)
-        put_points(pm, h * 256 + 8, tiles, -SHIFT, False)
-        put_points(pp, h * 256, tiles, SHIFT, False)
-    three_cells(range(1, 63), px, pm, p0, pp, fb)
+    plane = me // 8
+    for steps in STAGES:
+        inner = []
+        for step in steps:
+            here = lax.rem(plane + step, 4)
+            take(psem.at[here], recv2, (8 if step else 7) * 6)
+            for h in range(2):
+                tiles = [recv2[pl.ds(here * 128 + h * 3 + c, 8, stride=16), :] * SCALE for c in range(3)]
+                base = h * 256 + here * 64
+                put_points(px, base, tiles, 0.0, True)
+                put_points(p0, base, tiles, 0.0, False)
+                put_points(pm, base + 8, tiles, -SHIFT, False)
+                put_points(pp, base, tiles, SHIFT, False)
+            inner += [h * 32 + here * 8 + i for h in range(2) for i in range(1, 7)]
+        if steps is STAGES[-1]:
+            inner += [8 * i + j for i in range(8) for j in (0, 7)][1:-1]
+        three_cells(inner, px, pm, p0, pp, fb)
     for side in range(2):
         edge_copy(side, 0).wait_recv()
     put_points(pm, 0, [edge[3 + c : 4 + c, :] * SCALE for c in range(3)], -SHIFT, False)
@@ -393,7 +403,7 @@
             vm(2, 5, 5, BEADS, CELL), vm(5, BEADS, 768), vm(5, BEADS, 768),
             vm(2, 3, BEADS, CELL), vm(2, 2, 3, BEADS, CELL),
             *([vm(520, CELL)] * 5),
-            dma(8), dma(3), dma(3), dma(CHUNKS, 2, 2), dma(CHUNKS, 2, 2), dma(1), dma(2),
+            dma(8), dma(3), dma(3), dma(4), dma(CHUNKS, 2, 2), dma(CHUNKS, 2, 2), dma(1), dma(2),
         ],
         compiler_params=pltpu.CompilerParams(collective_id=0, has_side_effects=True),
     )(cells(positions), cells(momenta), cells(forces), modes_last(gle_drift), modes_last(gle_noise_mix), aux, kicks, jnp.asarray(constants()))

time: 32.9 us -> 32.3 us (0.982)
  Pallas kernels: 32 us -> 31.5 us
    pallas_call x1, Pallas kernels: 31.2 us -> 30.6 us  [on_device(): pl.pallas_call(body, out_shape=tuple((pltpu.VMEM(x, F32) for x in shapes)...]
where the time goes in v4:
time: 32.3 us; the launch traced here: 32.1 us
  Pallas kernels  31.5 us (98%)
  between operations  0.64 us (2%)
    pallas_call x1, Pallas kernels, on_device(): pl.pallas_call(body, out_shape=tuple((pltpu.VMEM(x, F32) for x in shapes)...  30.6 us
    pallas_call x1, Pallas kernels, on_device(): pl.pallas_call(hand_over, out_shape=tuple((jax.ShapeDtypeStruct(x, F32) f...  0.88 us

profile of v4, /device:TPU:1, one launch (start us, length us, event | category | flops | bytes accessed | tf_op | source)
XLA Modules:
  0.0 32.1 jit_solution(10902007420252158051)
XLA Ops:
  0.6 30.6 %shard_map.111 = (f32[3,64,128]{2,1,0:T(8,128)S(1)}, f32[3,64,128]{2,1,0:T(8,128)S(1)}, f32[3,64,128]{2,1,0:T(8,128)S(1)}, f32[768,128]{1,0:T(8,128)S(1)}) custom-call(f32[3,64,128]{2,1,0:T(8,128)} %bitcast.21, f32[3,64,128]{2,1,0:T(8,128)} %bitcast.22, f32[3,64,128]{2,1,0:T(8,128)} %bitcast.23, f32[5,5,32]{2,1,0:T(8,128)} %bitcast.24, ...), custom_call_target="tpu_custom_call" | custom-call | tf_op jit(solution)/shard_map/pallas_call | solution.py:394
  31.2 0.9 %shard_map.112 = (f32[3,64,128]{2,1,0:T(8,128)}, f32[3,64,128]{2,1,0:T(8,128)}, f32[3,64,128]{2,1,0:T(8,128)}, f32[768,128]{1,0:T(8,128)}) custom-call(f32[3,64,128]{2,1,0:T(8,128)S(1)} %get-tuple-element.12.refs_0_, f32[3,64,128]{2,1,0:T(8,128)S(1)} %get-tuple-element.13.refs_1_, f32[3,64,128]{2,1,0:T(8,128)S(1)} %get-tuple-element.14.refs_2_, ...), custom_call_target="tpu_custom_call" | custom-call | tf_op jit(solution)/shard_map/pallas_call | solution.py:410

commit v5 on v4

--- a/solution.py
+++ b/solution.py
@@ -184,14 +184,14 @@
             [(q_hbm, q), (p_hbm, p), (f_hbm, f), (dr_hbm, dr), (mx_hbm, mx), (aux_hbm, aux), (noise_hbm, noise), (cst_hbm, cst)]
         )
     ]
-    for c in loads:
-        c.start()
     barrier = pltpu.get_barrier_semaphore()
     up, down = lax.rem(s + 1, SPACES), lax.rem(s + SPACES - 1, SPACES)
 
-    for k in range(1, OWNERS):
-        pl.semaphore_signal(barrier, inc=1, device_id={"bead": lax.rem(me + k, OWNERS)}, device_id_type=MESH)
-
+    plane, place = me // 8, lax.rem(me, 8)
+    for step in ORDER1:
+        for k in range(0 if step else 1, 8):
+            peer = lax.rem(plane + step, 4) * 8 + lax.rem(place + k, 8)
+            pl.semaphore_signal(barrier, inc=1, device_id={"bead": peer}, device_id_type=MESH)
     first, last = me == 0, me == OWNERS - 1
 
     @pl.when(jnp.logical_or(first, last))
@@ -199,6 +199,8 @@
         there, bead = jnp.where(first, down, up), OWNERS - 1 - me
         pl.semaphore_signal(barrier, inc=1, device_id={"space": there, "bead": bead}, device_id_type=MESH)
 
+    for c in loads:
+        c.start()
     for c in loads[:3]:
         c.wait()
     for h in range(2):
@@ -333,7 +335,6 @@
     for c in halo:
         c.wait_send()
     sent()
-    plane = me // 8
     for steps in STAGES:
         inner = []
         for step in steps:

time: 32.3 us -> 32.2 us (level)
  no operation moved by 1% of the time
where the time goes in v5:
time: 32.2 us; the launch traced here: 32 us
  Pallas kernels  31.4 us (98%)
  between operations  0.64 us (2%)
    pallas_call x1, Pallas kernels, on_device(): pl.pallas_call(body, out_shape=tuple((pltpu.VMEM(x, F32) for x in shapes)...  30.5 us
    pallas_call x1, Pallas kernels, on_device(): pl.pallas_call(hand_over, out_shape=tuple((jax.ShapeDtypeStruct(x, F32) f...  0.88 us

profile of v5, /device:TPU:1, one launch (start us, length us, event | category | flops | bytes accessed | tf_op | source)
XLA Modules:
  0.0 32.0 jit_solution(16719144813700896275)
XLA Ops:
  0.6 30.5 %shard_map.111 = (f32[3,64,128]{2,1,0:T(8,128)S(1)}, f32[3,64,128]{2,1,0:T(8,128)S(1)}, f32[3,64,128]{2,1,0:T(8,128)S(1)}, f32[768,128]{1,0:T(8,128)S(1)}) custom-call(f32[3,64,128]{2,1,0:T(8,128)} %bitcast.21, f32[3,64,128]{2,1,0:T(8,128)} %bitcast.22, f32[3,64,128]{2,1,0:T(8,128)} %bitcast.23, f32[5,5,32]{2,1,0:T(8,128)} %bitcast.24, ...), custom_call_target="tpu_custom_call" | custom-call | tf_op jit(solution)/shard_map/pallas_call | solution.py:395
  31.1 0.9 %shard_map.112 = (f32[3,64,128]{2,1,0:T(8,128)}, f32[3,64,128]{2,1,0:T(8,128)}, f32[3,64,128]{2,1,0:T(8,128)}, f32[768,128]{1,0:T(8,128)}) custom-call(f32[3,64,128]{2,1,0:T(8,128)S(1)} %get-tuple-element.12.refs_0_, f32[3,64,128]{2,1,0:T(8,128)S(1)} %get-tuple-element.13.refs_1_, f32[3,64,128]{2,1,0:T(8,128)S(1)} %get-tuple-element.14.refs_2_, ...), custom_call_target="tpu_custom_call" | custom-call | tf_op jit(solution)/shard_map/pallas_call | solution.py:411

commit v6 on v5

--- a/solution.py
+++ b/solution.py
@@ -400,10 +400,10 @@
         scratch_shapes=[
             vm(3, 64, CELL), vm(3, 64, CELL), vm(3, 64, CELL), vm(5, 5, BEADS), vm(5, 5, BEADS),
             vm(768, CELL), vm(2, 5, 3, BEADS, 256), vm(5, BEADS, CELL),
-            vm(512, CELL), vm(512, CELL), vm(512, CELL), vm(512, CELL), vm(16, CELL),
+            vm(512, CELL), vm(512, CELL), vm(512, CELL), vm(512, CELL), vm(24, CELL),
             vm(2, 5, 5, BEADS, CELL), vm(5, BEADS, 768), vm(5, BEADS, 768),
             vm(2, 3, BEADS, CELL), vm(2, 2, 3, BEADS, CELL),
-            *([vm(520, CELL)] * 5),
+            *([vm(576, CELL)] * 5),
             dma(8), dma(3), dma(3), dma(4), dma(CHUNKS, 2, 2), dma(CHUNKS, 2, 2), dma(1), dma(2),
         ],
         compiler_params=pltpu.CompilerParams(collective_id=0, has_side_effects=True),

time: 32.2 us -> 32.2 us (level)
  no operation moved by 1% of the time
where the time goes in v6:
time: 32.2 us; the launch traced here: 32 us
  Pallas kernels  31.4 us (98%)
  between operations  0.64 us (2%)
    pallas_call x1, Pallas kernels, on_device(): pl.pallas_call(body, out_shape=tuple((pltpu.VMEM(x, F32) for x in shapes)...  30.5 us
    pallas_call x1, Pallas kernels, on_device(): pl.pallas_call(hand_over, out_shape=tuple((jax.ShapeDtypeStruct(x, F32) f...  0.88 us

profile of v6, /device:TPU:1, one launch (start us, length us, event | category | flops | bytes accessed | tf_op | source)
XLA Modules:
  0.0 32.0 jit_solution(4036228966328360546)
XLA Ops:
  0.6 30.5 %shard_map.111 = (f32[3,64,128]{2,1,0:T(8,128)S(1)}, f32[3,64,128]{2,1,0:T(8,128)S(1)}, f32[3,64,128]{2,1,0:T(8,128)S(1)}, f32[768,128]{1,0:T(8,128)S(1)}) custom-call(f32[3,64,128]{2,1,0:T(8,128)} %bitcast.21, f32[3,64,128]{2,1,0:T(8,128)} %bitcast.22, f32[3,64,128]{2,1,0:T(8,128)} %bitcast.23, f32[5,5,32]{2,1,0:T(8,128)} %bitcast.24, ...), custom_call_target="tpu_custom_call" | custom-call | tf_op jit(solution)/shard_map/pallas_call | solution.py:395
  31.1 0.9 %shard_map.112 = (f32[3,64,128]{2,1,0:T(8,128)}, f32[3,64,128]{2,1,0:T(8,128)}, f32[3,64,128]{2,1,0:T(8,128)}, f32[768,128]{1,0:T(8,128)}) custom-call(f32[3,64,128]{2,1,0:T(8,128)S(1)} %get-tuple-element.12.refs_0_, f32[3,64,128]{2,1,0:T(8,128)S(1)} %get-tuple-element.13.refs_1_, f32[3,64,128]{2,1,0:T(8,128)S(1)} %get-tuple-element.14.refs_2_, ...), custom_call_target="tpu_custom_call" | custom-call | tf_op jit(solution)/shard_map/pallas_call | solution.py:411
